TPU v7x, 128 devices: a whole 4x4x4 slice. The times are simulated.
128 devices in a mesh: sec: 4 (over x_hi, core), space: 32 (over z, x_lo, y).
Axes of the slice: x: 4 (x_hi: 2, x_lo: 2; x = x_hi * 2 + x_lo), y: 4, z: 4, core: 2. Of those that a mesh axis runs over, the one named last changes fastest.
Arguments:
- droplet_integrals: float32 [64, 5, 256, 2048], P('sec', None, 'space'), may hold values from -3 to 3, as said below
- flow_number_lengthwise: float32 [64], P('sec'), may hold values from -0.6 to 0.6
- flow_number_crosswise: float32 [64], P('sec'), may hold values from -0.35 to 0.35
- inflow_boundary_integrals: float32 [64, 5], P('sec'), may hold values from 0.2 to 2
- boundary_wall_indicator: int32 [256, 2048], P('space'), may hold values 0 or 1
- inflow_indicator: int32 [256, 2048], P('space'), may hold values 0 or 1
- collision_coefficient: float32 [64, 64], replicated, may hold values from 0.0005 to 0.008
- collision_target_share: float32 [64, 64], replicated, may hold values from 0 to 0.03
- evaporation_speed_stepwise: float32 [64], replicated, may hold values from 0.01 to 0.1
- thermal_factor: float32 [256, 2048], P('space', 'sec'), may hold values from 0.5 to 2
Outputs:
- spray: float32 [64, 5, 256, 2048], P(None, None, 'space', 'sec')
- gas_source: float32 [5, 256, 2048], P(None, 'space', 'sec')
Inputs may be any that keep to these rules, and one draw needn't show every extreme that they name: `droplet_integrals`: moment 0 (mass) is positive, 0.1 or more, in every section and cell.
All inputs are finite; a program needn't handle non-finite values. No bound on the sum of `boundary_wall_indicator` or of `inflow_indicator` on one device may be relied on, other than what follows from the above.
Results may differ from a plain program's by a relative error of at most 0.000084.
Values sent between devices are 32-bit elements; how exact they have to be, the bound alone decides.
A program may use at most 128 MiB of HBM per device.

v0:
```python
import functools

import jax
import jax.numpy as jnp
from jax import lax
from jax.experimental import pallas as pl
from jax.experimental.pallas import tpu as pltpu
from jax.sharding import PartitionSpec as P

SUB = 4
CHUNK = 4


def halo_rows(cells, width, outside):
    count = lax.axis_size("space")
    ends = count - 1
    dim = cells.ndim - 2
    head = lax.slice_in_dim(cells, 0, width, axis=dim)
    tail = lax.slice_in_dim(cells, cells.shape[dim] - width, cells.shape[dim], axis=dim)
    if outside:
        head, tail = 1 - head, 1 - tail
    west = lax.ppermute(tail, "space", [(i, i + 1) for i in range(ends)])
    east = lax.ppermute(head, "space", [(i + 1, i) for i in range(ends)])
    if outside:
        west, east = 1 - west, 1 - east
    return jnp.concatenate([cells, east, west], axis=dim)


def transport_kernel(
    groups, ux_ref, uy_ref, iv_ref, field_hbm, wall_ref, infl_ref, out_hbm,
    buf, slots, in_sems, send_sems, recv_sems, local_sem,
):
    group_size, moments, span, columns = field_hbm.shape
    rows = span - 2 * SUB
    block = columns // groups
    chunks = group_size // CHUNK
    me = lax.axis_index("sec")
    row = lax.axis_index("space")

    loads = []
    for c in range(chunks):
        load = pltpu.make_async_copy(
            field_hbm.at[pl.ds(c * CHUNK, CHUNK)], buf.at[pl.ds(c * CHUNK, CHUNK)], in_sems.at[c]
        )
        load.start()
        loads.append(load)

    barrier = pltpu.get_barrier_semaphore()
    for d in range(1, groups):
        pl.semaphore_signal(
            barrier, 1, device_id=(lax.rem(me + d, groups), row),
            device_id_type=pl.DeviceIdType.MESH,
        )
    pl.semaphore_wait(barrier, groups - 1)

    def cols_of(k):
        return pl.ds(pl.multiple_of(k * block, block), block)

    for c in range(chunks):
        loads[c].wait()

        def body(i, carry):
            s = c * CHUNK + i
            ux = ux_ref[s]
            uy = uy_ref[s]
            px = jnp.maximum(ux, 0.0)
            nx = jnp.minimum(ux, 0.0)
            py = jnp.maximum(uy, 0.0)
            ny = jnp.minimum(uy, 0.0)
            for m in range(moments):
                q = buf[s, m]
                iv = iv_ref[s * moments + m]
                for step in range(SUB):
                    col = lax.broadcasted_iota(jnp.int32, q.shape, 1)
                    west = pltpu.roll(q, 1, 0)
                    east = pltpu.roll(q, span - 1, 0)
                    south = jnp.where(col == 0, 0.0, pltpu.roll(q, 1, 1))
                    north = jnp.where(col == columns - 1, 0.0, pltpu.roll(q, columns - 1, 1))
                    t = q - px * (q - west) - nx * (east - q)
                    t = t - py * (q - south) - ny * (north - q)
                    t = jnp.where(infl_ref[...] > 0, iv, t)
                    q = jnp.where(wall_ref[...] > 0, 0.0, t)
                slots[s, m] = q[:rows]
            return carry

        lax.fori_loop(0, CHUNK, body, 0)

        part = pl.ds(c * CHUNK, CHUNK)
        for d in range(1, groups):
            k = lax.rem(me + d, groups)
            pltpu.make_async_remote_copy(
                src_ref=slots.at[part, :, :, cols_of(k)],
                dst_ref=out_hbm.at[pl.ds(me * group_size + c * CHUNK, CHUNK)],
                send_sem=send_sems.at[d - 1],
                recv_sem=recv_sems.at[d - 1],
                device_id=(k, row),
                device_id_type=pl.DeviceIdType.MESH,
            ).start()
        pltpu.make_async_copy(
            slots.at[part, :, :, cols_of(me)],
            out_hbm.at[pl.ds(me * group_size + c * CHUNK, CHUNK)],
            local_sem,
        ).start()

    pltpu.make_async_copy(
        slots.at[:, :, :, cols_of(me)], out_hbm.at[pl.ds(me * group_size, group_size)], local_sem
    ).wait()
    for d in range(1, groups):
        k = lax.rem(me + d, groups)
        source = lax.rem(me + groups - d, groups)
        pltpu.make_async_remote_copy(
            src_ref=slots.at[:, :, :, cols_of(k)],
            dst_ref=out_hbm.at[pl.ds(me * group_size, group_size)],
            send_sem=send_sems.at[d - 1],
            recv_sem=recv_sems.at[d - 1],
            device_id=(k, row),
            device_id_type=pl.DeviceIdType.MESH,
        ).wait_send()
        pltpu.make_async_remote_copy(
            src_ref=slots.at[:, :, :, cols_of(k)],
            dst_ref=out_hbm.at[pl.ds(source * group_size, group_size)],
            send_sem=send_sems.at[d - 1],
            recv_sem=recv_sems.at[d - 1],
            device_id=(k, row),
            device_id_type=pl.DeviceIdType.MESH,
        ).wait_recv()


def transport_exchange(speed_x, speed_y, inflow_value, field, wall_rows, inflow_rows):
    groups = lax.axis_size("sec")
    group_size, moments, span, columns = field.shape
    rows = span - 2 * SUB
    block = columns // groups
    smem = pl.BlockSpec(memory_space=pltpu.SMEM)
    vmem = pl.BlockSpec(memory_space=pltpu.VMEM)
    anywhere = pl.BlockSpec(memory_space=pl.ANY)
    flops = 30 * SUB * field.size
    return pl.pallas_call(
        functools.partial(transport_kernel, groups),
        out_shape=jax.ShapeDtypeStruct((groups * group_size, moments, rows, block), jnp.float32),
        in_specs=[smem, smem, smem, anywhere, vmem, vmem],
        out_specs=anywhere,
        scratch_shapes=[
            pltpu.VMEM((group_size, moments, span, columns), jnp.float32),
            pltpu.VMEM((group_size, moments, rows, columns), jnp.float32),
            pltpu.SemaphoreType.DMA((group_size // CHUNK,)),
            pltpu.SemaphoreType.DMA((groups - 1,)),
            pltpu.SemaphoreType.DMA((groups - 1,)),
            pltpu.SemaphoreType.DMA(()),
        ],
        compiler_params=pltpu.CompilerParams(
            collective_id=0, has_side_effects=True, vmem_limit_bytes=60 * 1024 * 1024
        ),
        cost_estimate=pl.CostEstimate(
            flops=flops, bytes_accessed=4 * (field.size * 2), transcendentals=0
        ),
    )(speed_x, speed_y, inflow_value.reshape(-1), field, wall_rows, inflow_rows)


def couple(cell_block, collision_coefficient, collision_target_share):
    mass_part = cell_block[:, 0]
    merge_rate = jnp.einsum(
        "sj,jxy->sxy", collision_coefficient, mass_part, precision=lax.Precision.HIGHEST
    )
    flux_terms = cell_block * merge_rate[:, None]
    gained = jnp.einsum(
        "sj,jmxy->smxy", collision_target_share, flux_terms, precision=lax.Precision.HIGHEST
    )
    return cell_block - flux_terms + gained


def shards(
    droplet_integrals,
    flow_number_lengthwise,
    flow_number_crosswise,
    inflow_boundary_integrals,
    boundary_wall_indicator,
    inflow_indicator,
    collision_coefficient,
    collision_target_share,
    evaporation_speed_stepwise,
    thermal_factor,
):
    field = halo_rows(droplet_integrals, SUB, False)
    wall_rows = halo_rows(boundary_wall_indicator, SUB, True)
    inflow_rows = halo_rows(inflow_indicator, SUB, False)
    cell_block = transport_exchange(
        flow_number_lengthwise, flow_number_crosswise, inflow_boundary_integrals,
        field, wall_rows, inflow_rows,
    )
    evaporated_quantity = (
        evaporation_speed_stepwise[:, None, None, None] * thermal_factor[None, None] * cell_block
    )
    gas_source = jnp.sum(evaporated_quantity, axis=0)
    remaining = cell_block - evaporated_quantity
    spray = couple(remaining, collision_coefficient, collision_target_share)
    return (spray, gas_source)


def solution(mesh):
    return jax.shard_map(
        shards,
        mesh=mesh,
        in_specs=(
            P("sec", None, "space", None),
            P("sec"),
            P("sec"),
            P("sec", None),
            P("space", None),
            P("space", None),
            P(),
            P(),
            P(),
            P("space", "sec"),
        ),
        out_specs=(P(None, None, "space", "sec"), P(None, "space", "sec")),
        check_vma=False,
    )
```

profile of v0, /device:TPU:97, one launch (start us, length us, event | category | flops | bytes accessed | tf_op | source)
XLA Modules:
  0.0 191.2 jit_solution(9667473188476265692)
XLA Ops:
  0.6 0.0 copy-start
  0.7 7.9 %fusion.5 = (f32[16,5,4,2048]{3,2,1,0:T(4,128)}, f32[16,5,4,2048]{3,2,1,0:T(4,128)}) fusion(f32[16,5,8,2048]{3,2,1,0:T(8,128)} %param.10), kind=kLoop, calls=%fused_computation.19 | loop fusion | bytes 10485760 | tf_op jit(solution)/shard_map/slice | solution.py:18
  8.6 5.4 %collective-permute-start = (f32[16,5,4,2048]{3,2,1,0:T(4,128)}, f32[16,5,4,2048]{3,2,1,0:T(4,128)}, u32[]{:S(2)}, u32[]{:S(2)}) collective-permute-start(f32[16,5,4,2048]{3,2,1,0:T(4,128)} %get-tuple-element.4), channel_id=1, source_target_pairs={{1,0},{2,1},{3,2},{4,3},{5,4},{6,5},{7,6},{8,7},{9,8},{10,9},{11,1... | collective-permute-start | bytes 7864328 | tf_op jit(solution)/shard_map/ppermute | solution.py:23
  14.0 1.9 %collective-permute-start.1 = (f32[16,5,4,2048]{3,2,1,0:T(4,128)}, f32[16,5,4,2048]{3,2,1,0:T(4,128)}, u32[]{:S(2)}, u32[]{:S(2)}) collective-permute-start(f32[16,5,4,2048]{3,2,1,0:T(4,128)} %get-tuple-element.5), channel_id=1, source_target_pairs={{0,1},{1,2},{2,3},{3,4},{4,5},{5,6},{6,7},{7,8},{8,9},{9,10},{10,1... | collective-permute-start | bytes 7864328 | tf_op jit(solution)/shard_map/ppermute | solution.py:22
  15.9 1.9 %collective-permute-start.3 = (s32[4,2048]{1,0:T(4,128)S(1)}, s32[4,2048]{1,0:T(4,128)S(1)}, u32[]{:S(2)}, u32[]{:S(2)}) collective-permute-start(s32[4,2048]{1,0:T(4,128)S(1)} %get-tuple-element.9), channel_id=1, source_target_pairs={{0,1},{1,2},{2,3},{3,4},{4,5},{5,6},{6,7},{7,8},{8,9},{9,10},{10,1... | collective-permute-start | bytes 98312 | tf_op jit(solution)/shard_map/ppermute | solution.py:22
  17.9 6.4 %collective-permute-start.2 = (s32[4,2048]{1,0:T(4,128)S(1)}, s32[4,2048]{1,0:T(4,128)S(1)}, u32[]{:S(2)}, u32[]{:S(2)}) collective-permute-start(s32[4,2048]{1,0:T(4,128)S(1)} %get-tuple-element.8), channel_id=1, source_target_pairs={{1,0},{2,1},{3,2},{4,3},{5,4},{6,5},{7,6},{8,7},{9,8},{10,9},{11,1... | collective-permute-start | bytes 98312 | tf_op jit(solution)/shard_map/ppermute | solution.py:23
  24.3 3.4 %collective-permute-start.4 = (s32[4,2048]{1,0:T(4,128)S(1)}, s32[4,2048]{1,0:T(4,128)S(1)}, u32[]{:S(2)}, u32[]{:S(2)}) collective-permute-start(s32[4,2048]{1,0:T(4,128)S(1)} %get-tuple-element.6), channel_id=1, source_target_pairs={{1,0},{2,1},{3,2},{4,3},{5,4},{6,5},{7,6},{8,7},{9,8},{10,9},{11,1... | collective-permute-start | bytes 98312 | tf_op jit(solution)/shard_map/ppermute | solution.py:23
  27.7 0.1 broadcast_multiply_fusion.1
  27.8 0.1 copy.17
  27.9 0.6 reshape.16.iv_ref
  28.5 48.8 %collective-permute-done.3 = s32[4,2048]{1,0:T(4,128)S(1)} collective-permute-done((s32[4,2048]{1,0:T(4,128)S(1)}, s32[4,2048]{1,0:T(4,128)S(1)}, u32[]{:S(2)}, u32[]{:S(2)}) %collective-permute-start.3) | collective-permute-done | bytes 32800 | tf_op jit(solution)/shard_map/ppermute | solution.py:22
  77.3 1.9 collective-permute-start.5
  79.3 0.7 pad_add_fusion.wall_ref
  79.9 5.0 %collective-permute-done.5 = s32[4,2048]{1,0:T(4,128)S(1)} collective-permute-done((s32[4,2048]{1,0:T(4,128)S(1)}, s32[4,2048]{1,0:T(4,128)S(1)}, u32[]{:S(2)}, u32[]{:S(2)}) %collective-permute-start.5) | collective-permute-done | bytes 32800 | tf_op jit(solution)/shard_map/ppermute | solution.py:22
  85.0 0.7 pad_add_fusion.1.infl_ref
  85.6 9.8 %pad_maximum_fusion.field_hbm = f32[16,5,16,2048]{3,2,1,0:T(8,128)} fusion(f32[16,5,4,2048]{3,2,1,0:T(4,128)} %collective-permute-done.1, f32[16,5,4,2048]{3,2,1,0:T(4,128)} %collective-permute-done, f32[16,5,8,2048]{3,2,1,0:T(8,128)} %param.10), kind=kLoop, calls=%fused_computation | loop fusion | flops 5242880 | bytes 20971520 | tf_op jit(solution)/shard_map/concatenate | solution.py:26
  95.4 72.5 %shard_map.113 = f32[64,5,8,512]{3,2,1,0:T(8,128)} custom-call(f32[16]{0:T(128)} %ux_ref.1, f32[16]{0:T(128)} %uy_ref.1, f32[80]{0:T(128)} %reshape.16.iv_ref, f32[16,5,16,2048]{3,2,1,0:T(8,128)} %pad_maximum_fusion.field_hbm, s32[16,2048]{1,0:T(8,128)} %pad_add_fusion.wall_ref, s32[16,2048]{1,0:T(8,128)} %pad_add_fusion.1.infl_ref), custom_call_target="tpu_custom_call" | custom-call | flops 314572800 | bytes 20971520 | tf_op jit(solution)/shard_map/pallas_call | solution.py:138
  167.9 4.3 %multiply_reduce_fusion = (f32[5,8,512]{2,1,0:T(8,128)}, f32[64,5,8,512]{3,2,1,0:T(8,128)S(1)}) fusion(f32[64,5,8,512]{3,2,1,0:T(8,128)} %shard_map.113, f32[64,8,512]{2,1,0:T(8,128)S(1)} %broadcast_multiply_fusion.1), kind=kLoop, calls=%fused_computation.1 | loop fusion | flops 3911680 | bytes 11616256 | tf_op jit(solution)/shard_map/reduce_sum | solution.py:194
  172.2 0.1 slice_bitcast_fusion
  172.3 1.7 convolution_bitcast_fusion
  174.0 0.6 copy.19
  174.6 0.9 broadcast_multiply_fusion
  175.6 9.2 %fusion = f32[5,8,512,64]{2,3,1,0:T(8,128)S(1)} fusion(f32[64,5,8,512]{3,2,1,0:T(8,128)S(1)} %broadcast_multiply_fusion, f32[64,64]{1,0:T(8,128)S(1)} %copy-done), kind=kOutput, calls=%fused_computation.4 | convolution fusion | flops 1006632960 | bytes 10502144 | tf_op jit(solution)/shard_map/sj,jmxy->smxy/dot_general | solution.py:166
  184.8 6.4 %bitcast_add_fusion = f32[64,5,8,512]{3,2,1,0:T(8,128)} fusion(f32[5,8,512,64]{2,3,1,0:T(8,128)S(1)} %fusion, f32[64,5,8,512]{3,2,1,0:T(8,128)S(1)} %get-tuple-element.3, f32[64,8,512]{2,1,0:T(8,128)S(1)} %copy.19), kind=kLoop, calls=%fused_computation.3 | loop fusion | flops 3932160 | bytes 16777216 | tf_op jit(solution)/shard_map/add | solution.py:169
  (21 shorter events, 0.1 us)
Async XLA Ops:
  0.6 175.0 %copy-start = (f32[64,64]{1,0:T(8,128)S(1)}, f32[64,64]{1,0:T(8,128)}, u32[]{:S(2)}) copy-start(f32[64,64]{1,0:T(8,128)} %param.17) | copy-start | bytes 49156
  0.6 15.3 %copy-start.1 = (s32[8,2048]{1,0:T(8,128)S(1)}, s32[8,2048]{1,0:T(8,128)}, u32[]{:S(2)}) copy-start(s32[8,2048]{1,0:T(8,128)} %param.14) | copy-start | bytes 196612
  0.7 23.6 %copy-start.2 = (s32[8,2048]{1,0:T(8,128)S(1)}, s32[8,2048]{1,0:T(8,128)}, u32[]{:S(2)}) copy-start(s32[8,2048]{1,0:T(8,128)} %param.15) | copy-start | bytes 196612
  0.7 27.0 %copy-start.6 = (f32[64]{0:T(128)S(1)}, f32[64]{0:T(128)}, u32[]{:S(2)}) copy-start(f32[64]{0:T(128)} %param.18) | copy-start | bytes 772
  0.7 27.0 %copy-start.4 = (f32[8,512]{1,0:T(8,128)S(1)}, f32[8,512]{1,0:T(8,128)}, u32[]{:S(2)}) copy-start(f32[8,512]{1,0:T(8,128)} %param.19) | copy-start | bytes 49156
  0.7 27.1 %copy-start.5 = (f32[16,5]{0,1:T(8,128)S(1)}, f32[16,5]{0,1:T(8,128)}, u32[]{:S(2)}) copy-start(f32[16,5]{0,1:T(8,128)} %param.13) | copy-start | bytes 964
  8.6 77.1 %collective-permute-start = (f32[16,5,4,2048]{3,2,1,0:T(4,128)}, f32[16,5,4,2048]{3,2,1,0:T(4,128)}, u32[]{:S(2)}, u32[]{:S(2)}) collective-permute-start(f32[16,5,4,2048]{3,2,1,0:T(4,128)} %get-tuple-element.4), channel_id=1, source_target_pairs={{1,0},{2,1},{3,2},{4,3},{5,4},{6,5},{7,6},{8,7},{9,8},{10,9},{11,1... | collective-permute-start | bytes 7864328 | tf_op jit(solution)/shard_map/ppermute | solution.py:23
  14.0 71.7 %collective-permute-start.1 = (f32[16,5,4,2048]{3,2,1,0:T(4,128)}, f32[16,5,4,2048]{3,2,1,0:T(4,128)}, u32[]{:S(2)}, u32[]{:S(2)}) collective-permute-start(f32[16,5,4,2048]{3,2,1,0:T(4,128)} %get-tuple-element.5), channel_id=1, source_target_pairs={{0,1},{1,2},{2,3},{3,4},{4,5},{5,6},{6,7},{7,8},{8,9},{9,10},{10,1... | collective-permute-start | bytes 7864328 | tf_op jit(solution)/shard_map/ppermute | solution.py:22
  15.9 61.4 %collective-permute-start.3 = (s32[4,2048]{1,0:T(4,128)S(1)}, s32[4,2048]{1,0:T(4,128)S(1)}, u32[]{:S(2)}, u32[]{:S(2)}) collective-permute-start(s32[4,2048]{1,0:T(4,128)S(1)} %get-tuple-element.9), channel_id=1, source_target_pairs={{0,1},{1,2},{2,3},{3,4},{4,5},{5,6},{6,7},{7,8},{8,9},{9,10},{10,1... | collective-permute-start | bytes 98312 | tf_op jit(solution)/shard_map/ppermute | solution.py:22
  17.9 61.4 %collective-permute-start.2 = (s32[4,2048]{1,0:T(4,128)S(1)}, s32[4,2048]{1,0:T(4,128)S(1)}, u32[]{:S(2)}, u32[]{:S(2)}) collective-permute-start(s32[4,2048]{1,0:T(4,128)S(1)} %get-tuple-element.8), channel_id=1, source_target_pairs={{1,0},{2,1},{3,2},{4,3},{5,4},{6,5},{7,6},{8,7},{9,8},{10,9},{11,1... | collective-permute-start | bytes 98312 | tf_op jit(solution)/shard_map/ppermute | solution.py:23
  24.3 55.7 %collective-permute-start.4 = (s32[4,2048]{1,0:T(4,128)S(1)}, s32[4,2048]{1,0:T(4,128)S(1)}, u32[]{:S(2)}, u32[]{:S(2)}) collective-permute-start(s32[4,2048]{1,0:T(4,128)S(1)} %get-tuple-element.6), channel_id=1, source_target_pairs={{1,0},{2,1},{3,2},{4,3},{5,4},{6,5},{7,6},{8,7},{9,8},{10,9},{11,1... | collective-permute-start | bytes 98312 | tf_op jit(solution)/shard_map/ppermute | solution.py:23
  77.3 7.7 %collective-permute-start.5 = (s32[4,2048]{1,0:T(4,128)S(1)}, s32[4,2048]{1,0:T(4,128)S(1)}, u32[]{:S(2)}, u32[]{:S(2)}) collective-permute-start(s32[4,2048]{1,0:T(4,128)S(1)} %get-tuple-element.7), channel_id=1, source_target_pairs={{0,1},{1,2},{2,3},{3,4},{4,5},{5,6},{6,7},{7,8},{8,9},{9,10},{10,1... | collective-permute-start | bytes 98312 | tf_op jit(solution)/shard_map/ppermute | solution.py:22
  167.9 4.4 %copy-start.3 = (f32[64,64]{1,0:T(8,128)S(1)}, f32[64,64]{1,0:T(8,128)}, u32[]{:S(2)}) copy-start(f32[64,64]{1,0:T(8,128)} %param.16) | copy-start | bytes 49156
where the time goes:
time: 191 us
  Pallas kernels  72.5 us (38%)
  waiting for transfers between devices  53.8 us (28%)
  other arithmetic  22.9 us (12%)
  starting transfers between devices  20.9 us (11%)
  matrix products  10.9 us (6%)
  local copies, waits for them, and re-layouts  9.28 us (5%)
    pallas_call x1, Pallas kernels, transport_exchange(): pl.pallas_call(functools.partial(transport_kernel, groups), out_shape=jax...  72.5 us
    ppermute x3, waiting for transfers between devices, halo_rows(): west = lax.ppermute(tail, 'space', [(i, i + 1) for i in range(ends)])  53.8 us
    ppermute x3, starting transfers between devices, halo_rows(): east = lax.ppermute(head, 'space', [(i + 1, i) for i in range(ends)])  15.1 us
    concatenate x3, other arithmetic, halo_rows(): return jnp.concatenate([cells, east, west], axis=dim)  11.1 us
    dot_general x1, matrix products, couple(): jnp.einsum('sj,jmxy->smxy', collision_target_share, flux_terms, precision...  9.22 us
    slice x2, local copies, waits for them, and re-layouts, halo_rows(): head = lax.slice_in_dim(cells, 0, width, axis=dim)  7.88 us
    add x1, other arithmetic, couple(): return cell_block - flux_terms + gained  6.4 us
    ppermute x3, starting transfers between devices, halo_rows(): west = lax.ppermute(tail, 'space', [(i, i + 1) for i in range(ends)])  5.75 us
  transfers between devices with their start and end apart: 6, of which 2 were waited for; matrix products, arithmetic and copies ran while one was open for 1% of the time, Pallas kernels for 0%

commit v1 on v0

v1 whole, which is shorter than its diff:
```python
import functools

import jax
import jax.numpy as jnp
from jax import lax
from jax.experimental import pallas as pl
from jax.experimental.pallas import tpu as pltpu
from jax.sharding import PartitionSpec as P

SUB = 4
CHUNK = 4
MESH = pl.DeviceIdType.MESH


def transport_kernel(
    groups, lines,
    ux_ref, uy_ref, iv_ref, field_hbm, wall_ref, infl_ref,
    out_hbm,
    local, halo, wall_halo, infl_halo, slots,
    load_sems, halo_recv, halo_send, mask_recv, mask_send, send_sems, recv_sems, local_sem,
):
    group_size, moments, rows, columns = field_hbm.shape
    span = 2 * rows
    block = columns // groups
    chunks = group_size // CHUNK
    me = lax.axis_index("sec")
    row = lax.axis_index("space")
    has_west = (row + lines - 1) // lines
    has_east = 1 - row // (lines - 1)
    west = (me, row - 1)
    east = (me, row + 1)
    first = pl.ds(0, SUB)
    last = pl.ds(SUB, SUB)

    loads = []
    for c in range(chunks):
        part = pl.ds(c * CHUNK, CHUNK)
        load = pltpu.make_async_copy(field_hbm.at[part], local.at[part], load_sems.at[c])
        load.start()
        loads.append(load)

    @pl.when(row == 0)
    def _():
        halo[:, :, last, :] = jnp.zeros((group_size, moments, SUB, columns), jnp.float32)
        wall_halo[last, :] = jnp.ones((SUB, columns), jnp.int32)
        infl_halo[last, :] = jnp.zeros((SUB, columns), jnp.int32)

    @pl.when(row == lines - 1)
    def _():
        halo[:, :, first, :] = jnp.zeros((group_size, moments, SUB, columns), jnp.float32)
        wall_halo[first, :] = jnp.ones((SUB, columns), jnp.int32)
        infl_halo[first, :] = jnp.zeros((SUB, columns), jnp.int32)

    barrier = pltpu.get_barrier_semaphore()
    for d in range(1, groups):
        pl.semaphore_signal(barrier, 1, device_id=(lax.rem(me + d, groups), row), device_id_type=MESH)

    @pl.when(row > 0)
    def _():
        pl.semaphore_signal(barrier, 1, device_id=west, device_id_type=MESH)

    @pl.when(row < lines - 1)
    def _():
        pl.semaphore_signal(barrier, 1, device_id=east, device_id_type=MESH)

    pl.semaphore_wait(barrier, groups - 1 + has_west + has_east)

    def halo_copy(src, dst, direction, sem_recv, sem_send):
        return pltpu.make_async_remote_copy(
            src_ref=src, dst_ref=dst, send_sem=sem_send, recv_sem=sem_recv,
            device_id=west if direction == 0 else east, device_id_type=MESH,
        )

    def field_halo(c, direction):
        part = pl.ds(c * CHUNK, CHUNK)
        if direction == 0:
            return halo_copy(field_hbm.at[part, :, first, :], halo.at[part, :, first, :], 0,
                             halo_recv.at[0, c], halo_send.at[0])
        return halo_copy(field_hbm.at[part, :, pl.ds(rows - SUB, SUB), :], halo.at[part, :, last, :], 1,
                         halo_recv.at[1, c], halo_send.at[1])

    def mask_halo(ref, store, k, direction):
        if direction == 0:
            return halo_copy(ref.at[first, :], store.at[first, :], 0, mask_recv.at[k, 0], mask_send.at[k, 0])
        return halo_copy(ref.at[pl.ds(rows - SUB, SUB), :], store.at[last, :], 1,
                         mask_recv.at[k, 1], mask_send.at[k, 1])

    @pl.when(row > 0)
    def _():
        mask_halo(wall_ref, wall_halo, 0, 0).start()
        mask_halo(infl_ref, infl_halo, 1, 0).start()
        for c in range(chunks):
            field_halo(c, 0).start()

    @pl.when(row < lines - 1)
    def _():
        mask_halo(wall_ref, wall_halo, 0, 1).start()
        mask_halo(infl_ref, infl_halo, 1, 1).start()
        for c in range(chunks):
            field_halo(c, 1).start()

    @pl.when(row < lines - 1)
    def _():
        mask_halo(wall_ref, wall_halo, 0, 0).wait_recv()
        mask_halo(infl_ref, infl_halo, 1, 0).wait_recv()

    @pl.when(row > 0)
    def _():
        mask_halo(wall_ref, wall_halo, 0, 1).wait_recv()
        mask_halo(infl_ref, infl_halo, 1, 1).wait_recv()

    def cols_of(k):
        return pl.ds(pl.multiple_of(k * block, block), block)

    for c in range(chunks):
        loads[c].wait()

        @pl.when(row < lines - 1)
        def _():
            field_halo(c, 0).wait_recv()

        @pl.when(row > 0)
        def _():
            field_halo(c, 1).wait_recv()

        def body(i, carry):
            s = c * CHUNK + i
            ux = ux_ref[s]
            uy = uy_ref[s]
            px = jnp.maximum(ux, 0.0)
            nx = jnp.minimum(ux, 0.0)
            py = jnp.maximum(uy, 0.0)
            ny = jnp.minimum(uy, 0.0)
            for m in range(moments):
                q = jnp.concatenate([local[s, m], halo[s, m]], axis=0)
                iv = iv_ref[s * moments + m]
                for step in range(SUB):
                    col = lax.broadcasted_iota(jnp.int32, q.shape, 1)
                    western = pltpu.roll(q, 1, 0)
                    eastern = pltpu.roll(q, span - 1, 0)
                    southern = jnp.where(col == 0, 0.0, pltpu.roll(q, 1, 1))
                    northern = jnp.where(col == columns - 1, 0.0, pltpu.roll(q, columns - 1, 1))
                    t = q - px * (q - western) - nx * (eastern - q)
                    t = t - py * (q - southern) - ny * (northern - q)
                    inflow_rows = jnp.concatenate([infl_ref[...], infl_halo[...]], axis=0)
                    wall_rows = jnp.concatenate([wall_ref[...], wall_halo[...]], axis=0)
                    t = jnp.where(inflow_rows > 0, iv, t)
                    q = jnp.where(wall_rows > 0, 0.0, t)
                slots[s, m] = q[:rows]
            return carry

        lax.fori_loop(0, CHUNK, body, 0)

        part = pl.ds(c * CHUNK, CHUNK)
        for d in range(1, groups):
            k = lax.rem(me + d, groups)
            pltpu.make_async_remote_copy(
                src_ref=slots.at[part, :, :, cols_of(k)],
                dst_ref=out_hbm.at[pl.ds(me * group_size + c * CHUNK, CHUNK)],
                send_sem=send_sems.at[d - 1],
                recv_sem=recv_sems.at[d - 1],
                device_id=(k, row),
                device_id_type=MESH,
            ).start()
        pltpu.make_async_copy(
            slots.at[part, :, :, cols_of(me)],
            out_hbm.at[pl.ds(me * group_size + c * CHUNK, CHUNK)],
            local_sem,
        ).start()

    @pl.when(row > 0)
    def _():
        mask_halo(wall_ref, wall_halo, 0, 0).wait_send()
        mask_halo(infl_ref, infl_halo, 1, 0).wait_send()
        halo_copy(field_hbm.at[:, :, first, :], halo.at[:, :, first, :], 0,
                  halo_recv.at[0, 0], halo_send.at[0]).wait_send()

    @pl.when(row < lines - 1)
    def _():
        mask_halo(wall_ref, wall_halo, 0, 1).wait_send()
        mask_halo(infl_ref, infl_halo, 1, 1).wait_send()
        halo_copy(field_hbm.at[:, :, pl.ds(rows - SUB, SUB), :], halo.at[:, :, last, :], 1,
                  halo_recv.at[1, 0], halo_send.at[1]).wait_send()

    pltpu.make_async_copy(
        slots.at[:, :, :, cols_of(me)], out_hbm.at[pl.ds(me * group_size, group_size)], local_sem
    ).wait()
    for d in range(1, groups):
        k = lax.rem(me + d, groups)
        source = lax.rem(me + groups - d, groups)
        pltpu.make_async_remote_copy(
            src_ref=slots.at[:, :, :, cols_of(k)],
            dst_ref=out_hbm.at[pl.ds(me * group_size, group_size)],
            send_sem=send_sems.at[d - 1],
            recv_sem=recv_sems.at[d - 1],
            device_id=(k, row),
            device_id_type=MESH,
        ).wait_send()
        pltpu.make_async_remote_copy(
            src_ref=slots.at[:, :, :, cols_of(k)],
            dst_ref=out_hbm.at[pl.ds(source * group_size, group_size)],
            send_sem=send_sems.at[d - 1],
            recv_sem=recv_sems.at[d - 1],
            device_id=(k, row),
            device_id_type=MESH,
        ).wait_recv()


def transport_exchange(speed_x, speed_y, inflow_value, field, wall_rows, inflow_rows):
    groups = lax.axis_size("sec")
    lines = lax.axis_size("space")
    group_size, moments, rows, columns = field.shape
    block = columns // groups
    chunks = group_size // CHUNK
    smem = pl.BlockSpec(memory_space=pltpu.SMEM)
    vmem = pl.BlockSpec(memory_space=pltpu.VMEM)
    anywhere = pl.BlockSpec(memory_space=pl.ANY)
    flops = 60 * SUB * field.size
    return pl.pallas_call(
        functools.partial(transport_kernel, groups, lines),
        out_shape=jax.ShapeDtypeStruct((groups * group_size, moments, rows, block), jnp.float32),
        in_specs=[smem, smem, smem, anywhere, vmem, vmem],
        out_specs=anywhere,
        scratch_shapes=[
            pltpu.VMEM((group_size, moments, rows, columns), jnp.float32),
            pltpu.VMEM((group_size, moments, rows, columns), jnp.float32),
            pltpu.VMEM((rows, columns), jnp.int32),
            pltpu.VMEM((rows, columns), jnp.int32),
            pltpu.VMEM((group_size, moments, rows, columns), jnp.float32),
            pltpu.SemaphoreType.DMA((chunks,)),
            pltpu.SemaphoreType.DMA((2, chunks)),
            pltpu.SemaphoreType.DMA((2,)),
            pltpu.SemaphoreType.DMA((2, 2)),
            pltpu.SemaphoreType.DMA((2, 2)),
            pltpu.SemaphoreType.DMA((groups - 1,)),
            pltpu.SemaphoreType.DMA((groups - 1,)),
            pltpu.SemaphoreType.DMA(()),
        ],
        compiler_params=pltpu.CompilerParams(
            collective_id=0, has_side_effects=True, vmem_limit_bytes=60 * 1024 * 1024
        ),
        cost_estimate=pl.CostEstimate(
            flops=flops, bytes_accessed=4 * (field.size * 2), transcendentals=0
        ),
    )(speed_x, speed_y, inflow_value.reshape(-1), field, wall_rows, inflow_rows)


def couple(cell_block, collision_coefficient, collision_target_share):
    mass_part = cell_block[:, 0]
    merge_rate = jnp.einsum(
        "sj,jxy->sxy", collision_coefficient, mass_part, precision=lax.Precision.HIGHEST
    )
    flux_terms = cell_block * merge_rate[:, None]
    gained = jnp.einsum(
        "sj,jmxy->smxy", collision_target_share, flux_terms, precision=lax.Precision.HIGHEST
    )
    return cell_block - flux_terms + gained


def shards(
    droplet_integrals,
    flow_number_lengthwise,
    flow_number_crosswise,
    inflow_boundary_integrals,
    boundary_wall_indicator,
    inflow_indicator,
    collision_coefficient,
    collision_target_share,
    evaporation_speed_stepwise,
    thermal_factor,
):
    cell_block = transport_exchange(
        flow_number_lengthwise, flow_number_crosswise, inflow_boundary_integrals,
        droplet_integrals, boundary_wall_indicator, inflow_indicator,
    )
    evaporated_quantity = (
        evaporation_speed_stepwise[:, None, None, None] * thermal_factor[None, None] * cell_block
    )
    gas_source = jnp.sum(evaporated_quantity, axis=0)
    remaining = cell_block - evaporated_quantity
    spray = couple(remaining, collision_coefficient, collision_target_share)
    return (spray, gas_source)


def solution(mesh):
    return jax.shard_map(
        shards,
        mesh=mesh,
        in_specs=(
            P("sec", None, "space", None),
            P("sec"),
            P("sec"),
            P("sec", None),
            P("space", None),
            P("space", None),
            P(),
            P(),
            P(),
            P("space", "sec"),
        ),
        out_specs=(P(None, None, "space", "sec"), P(None, "space", "sec")),
        check_vma=False,
    )
```

time: 191 us -> 149 us (0.78)
  waiting for transfers between devices: 53.8 us -> 0 us
  Pallas kernels: 72.5 us -> 122 us
  starting transfers between devices: 20.9 us -> 0 us
  other arithmetic: 22.9 us -> 12.5 us
  local copies, waits for them, and re-layouts: 9.28 us -> 2.07 us
    ppermute x6 -> x0, waiting for transfers between devices: 53.8 us -> none  [the longest x3 53.8 us: halo_rows(): west = lax.ppermute(tail, 'space', [(i, i + 1) for i in range(ends)])]
    pallas_call x1, Pallas kernels: 72.5 us -> 122 us  [transport_exchange(): pl.pallas_call(functools.partial(transport_kernel, groups, lines), out_sh...]
    ppermute x6 -> x0, starting transfers between devices: 20.9 us -> none  [the longest x3 15.1 us: halo_rows(): east = lax.ppermute(head, 'space', [(i + 1, i) for i in range(ends)])]
    concatenate x3 -> x0, other arithmetic: 11.1 us -> none  [halo_rows(): return jnp.concatenate([cells, east, west], axis=dim)]
    slice x2 -> x0, local copies, waits for them, and re-layouts: 7.88 us -> none  [halo_rows(): head = lax.slice_in_dim(cells, 0, width, axis=dim)]
  transfers between devices with their start and end apart: 6 -> 0, of which waited for: 2 -> 0; matrix products, arithmetic and copies ran while one was open for 1% -> 0% of each run, Pallas kernels for 0% -> 0%
where the time goes in v1:
time: 149 us; the launch traced here: 148 us
  Pallas kernels  122 us (82%)
  other arithmetic  12.5 us (8%)
  matrix products  10.9 us (7%)
  local copies, waits for them, and re-layouts  2.07 us (1%)
    pallas_call x1, Pallas kernels, transport_exchange(): pl.pallas_call(functools.partial(transport_kernel, groups, lines), out_sh...  122 us
    dot_general x1, matrix products, couple(): jnp.einsum('sj,jmxy->smxy', collision_target_share, flux_terms, precision...  9.21 us
    add x1, other arithmetic, couple(): return cell_block - flux_terms + gained  6.4 us
    reduce_sum x1, other arithmetic, shards(): gas_source = jnp.sum(evaporated_quantity, axis=0)  4.28 us

profile of v1, /device:TPU:97, one launch (start us, length us, event | category | flops | bytes accessed | tf_op | source)
XLA Modules:
  0.0 148.2 jit_solution(17603740165004503545)
XLA Ops:
  0.6 0.0 copy-start
  0.6 0.8 copy.17
  1.4 0.6 reshape.16.iv_ref
  2.0 0.9 broadcast_multiply_fusion.1
  2.9 122.0 %shard_map.113 = f32[64,5,8,512]{3,2,1,0:T(8,128)} custom-call(f32[16]{0:T(128)} %ux_ref.1, f32[16]{0:T(128)} %uy_ref.1, f32[80]{0:T(128)} %reshape.16.iv_ref, f32[16,5,8,2048]{3,2,1,0:T(8,128)} %field_hbm.1, s32[8,2048]{1,0:T(8,128)} %wall_ref.1, s32[8,2048]{1,0:T(8,128)} %infl_ref.1), custom_call_target="tpu_custom_call" | custom-call | flops 314572800 | bytes 10485760 | tf_op jit(solution)/shard_map/pallas_call | solution.py:219
  124.9 0.0 copy-start.1
  124.9 4.3 %multiply_reduce_fusion = (f32[5,8,512]{2,1,0:T(8,128)}, f32[64,5,8,512]{3,2,1,0:T(8,128)S(1)}) fusion(f32[64,5,8,512]{3,2,1,0:T(8,128)} %shard_map.113, f32[64,8,512]{2,1,0:T(8,128)S(1)} %broadcast_multiply_fusion.1), kind=kLoop, calls=%fused_computation | loop fusion | flops 3911680 | bytes 11616256 | tf_op jit(solution)/shard_map/reduce_sum | solution.py:279
  129.2 0.1 slice_bitcast_fusion
  129.3 0.0 copy-done.1
  129.3 1.7 %convolution_bitcast_fusion = f32[64,8,512]{2,0,1:T(8,128)S(1)} fusion(f32[64,8,512]{2,1,0:T(8,128)S(1)} %slice_bitcast_fusion, f32[64,64]{1,0:T(8,128)S(1)} %copy-done.1), kind=kOutput, calls=%fused_computation.6 | convolution fusion | flops 201326592 | bytes 2113536 | tf_op jit(solution)/shard_map/sj,jxy->sxy/dot_general | solution.py:250
  131.0 0.6 copy.19
  131.6 0.9 broadcast_multiply_fusion
  132.6 0.0 copy-done
  132.6 9.2 %fusion = f32[5,8,512,64]{2,3,1,0:T(8,128)S(1)} fusion(f32[64,5,8,512]{3,2,1,0:T(8,128)S(1)} %broadcast_multiply_fusion, f32[64,64]{1,0:T(8,128)S(1)} %copy-done), kind=kOutput, calls=%fused_computation.3 | convolution fusion | flops 1006632960 | bytes 10502144 | tf_op jit(solution)/shard_map/sj,jmxy->smxy/dot_general | solution.py:254
  141.8 6.4 %bitcast_add_fusion = f32[64,5,8,512]{3,2,1,0:T(8,128)} fusion(f32[5,8,512,64]{2,3,1,0:T(8,128)S(1)} %fusion, f32[64,5,8,512]{3,2,1,0:T(8,128)S(1)} %get-tuple-element.3, f32[64,8,512]{2,1,0:T(8,128)S(1)} %copy.19), kind=kLoop, calls=%fused_computation.2 | loop fusion | flops 3932160 | bytes 16777216 | tf_op jit(solution)/shard_map/add | solution.py:257
Async XLA Ops:
  0.6 132.0 %copy-start = (f32[64,64]{1,0:T(8,128)S(1)}, f32[64,64]{1,0:T(8,128)}, u32[]{:S(2)}) copy-start(f32[64,64]{1,0:T(8,128)} %param.17) | copy-start | bytes 49156
  124.9 4.4 %copy-start.1 = (f32[64,64]{1,0:T(8,128)S(1)}, f32[64,64]{1,0:T(8,128)}, u32[]{:S(2)}) copy-start(f32[64,64]{1,0:T(8,128)} %param.16) | copy-start | bytes 49156

commit v2 on v1

--- a/solution.py
+++ b/solution.py
@@ -245,16 +245,60 @@
     )(speed_x, speed_y, inflow_value.reshape(-1), field, wall_rows, inflow_rows)
 
 
-def couple(cell_block, collision_coefficient, collision_target_share):
-    mass_part = cell_block[:, 0]
-    merge_rate = jnp.einsum(
-        "sj,jxy->sxy", collision_coefficient, mass_part, precision=lax.Precision.HIGHEST
-    )
-    flux_terms = cell_block * merge_rate[:, None]
-    gained = jnp.einsum(
-        "sj,jmxy->smxy", collision_target_share, flux_terms, precision=lax.Precision.HIGHEST
-    )
-    return cell_block - flux_terms + gained
+def post_kernel(rate_ref, tf_ref, coef_ref, share_ref, x_ref, spray_ref, gas_ref):
+    span, _ = gas_ref.shape
+    rows = tf_ref.shape[0]
+    moments = span // rows
+    sections = rate_ref.shape[0]
+    highest = lax.Precision.HIGHEST
+    rate = rate_ref[...]
+    coef = coef_ref[...]
+    share = share_ref[...]
+    for r in range(rows):
+        factor = rate * tf_ref[pl.ds(r, 1), :]
+        remaining = []
+        for m in range(moments):
+            x = x_ref[pl.ds(m * rows + r, sections, stride=span), :]
+            evaporated = factor * x
+            gas_ref[pl.ds(m * rows + r, 1), :] = jnp.sum(evaporated, axis=0, keepdims=True)
+            remaining.append(x - evaporated)
+        merge_rate = jnp.dot(coef, remaining[0], precision=highest, preferred_element_type=jnp.float32)
+        for m in range(moments):
+            flux = remaining[m] * merge_rate
+            gained = jnp.dot(share, flux, precision=highest, preferred_element_type=jnp.float32)
+            spray_ref[pl.ds(m * rows + r, sections, stride=span), :] = remaining[m] - flux + gained
+
+
+def evaporate_couple(cell_block, rates, thermal_factor, coefficient, share):
+    sections, moments, rows, block = cell_block.shape
+    strip = 128
+    span = moments * rows
+    flat = cell_block.reshape(sections * span, block)
+    full = lambda shape: pl.BlockSpec(shape, lambda i: (0, 0))
+    spray, gas = pl.pallas_call(
+        post_kernel,
+        grid=(block // strip,),
+        in_specs=[
+            full((sections, 1)),
+            pl.BlockSpec((rows, strip), lambda i: (0, i)),
+            full((sections, sections)),
+            full((sections, sections)),
+            pl.BlockSpec((sections * span, strip), lambda i: (0, i)),
+        ],
+        out_specs=[
+            pl.BlockSpec((sections * span, strip), lambda i: (0, i)),
+            pl.BlockSpec((span, strip), lambda i: (0, i)),
+        ],
+        out_shape=[
+            jax.ShapeDtypeStruct((sections * span, block), jnp.float32),
+            jax.ShapeDtypeStruct((span, block), jnp.float32),
+        ],
+        cost_estimate=pl.CostEstimate(
+            flops=2 * sections * sections * flat.size // sections * (moments + 1) // moments * 6,
+            bytes_accessed=8 * flat.size, transcendentals=0,
+        ),
+    )(rates.reshape(sections, 1), thermal_factor, coefficient, share, flat)
+    return spray.reshape(sections, moments, rows, block), gas.reshape(moments, rows, block)
 
 
 def shards(
@@ -273,12 +317,10 @@
         flow_number_lengthwise, flow_number_crosswise, inflow_boundary_integrals,
         droplet_integrals, boundary_wall_indicator, inflow_indicator,
     )
-    evaporated_quantity = (
-        evaporation_speed_stepwise[:, None, None, None] * thermal_factor[None, None] * cell_block
+    spray, gas_source = evaporate_couple(
+        cell_block, evaporation_speed_stepwise, thermal_factor,
+        collision_coefficient, collision_target_share,
     )
-    gas_source = jnp.sum(evaporated_quantity, axis=0)
-    remaining = cell_block - evaporated_quantity
-    spray = couple(remaining, collision_coefficient, collision_target_share)
     return (spray, gas_source)
 
 

time: 149 us -> 139 us (0.933)
  Pallas kernels: 122 us -> 135 us
  other arithmetic: 12.5 us -> 0 us
  matrix products: 10.9 us -> 0 us
    pallas_call x0 -> x1, Pallas kernels: none -> 13.4 us  [evaporate_couple(): pl.pallas_call(post_kernel, grid=(block // strip,), in_specs=[full((secti...]
    dot_general x2 -> x0, matrix products: 10.9 us -> none  [the longest x1 9.21 us: couple(): jnp.einsum('sj,jmxy->smxy', collision_target_share, flux_terms, precision...]
    add x1 -> x0, other arithmetic: 6.4 us -> none  [couple(): return cell_block - flux_terms + gained]
    reduce_sum x1 -> x0, other arithmetic: 4.28 us -> none  [shards(): gas_source = jnp.sum(evaporated_quantity, axis=0)]
    mul x2 -> x0, other arithmetic: 1.78 us -> none  [the longest x1 0.93 us: couple(): flux_terms = cell_block * merge_rate[:, None]]
where the time goes in v2:
time: 139 us
  Pallas kernels  135 us (97%)
  local copies, waits for them, and re-layouts  2.72 us (2%)
    pallas_call x1, Pallas kernels, transport_exchange(): pl.pallas_call(functools.partial(transport_kernel, groups, lines), out_sh...  122 us
    pallas_call x1, Pallas kernels, evaporate_couple(): pl.pallas_call(post_kernel, grid=(block // strip,), in_specs=[full((secti...  13.4 us

profile of v2, /device:TPU:97, one launch (start us, length us, event | category | flops | bytes accessed | tf_op | source)
XLA Modules:
  0.0 138.7 jit_solution(7349671801256515952)
XLA Ops:
  0.6 0.8 copy.14
  1.4 0.6 reshape.20.iv_ref
  2.0 1.4 copy.15.rate_ref
  3.4 122.0 %shard_map.113 = f32[64,5,8,512]{3,2,1,0:T(8,128)} custom-call(f32[16]{0:T(128)} %ux_ref.1, f32[16]{0:T(128)} %uy_ref.1, f32[80]{0:T(128)} %reshape.20.iv_ref, f32[16,5,8,2048]{3,2,1,0:T(8,128)} %field_hbm.1, s32[8,2048]{1,0:T(8,128)} %wall_ref.1, s32[8,2048]{1,0:T(8,128)} %infl_ref.1), custom_call_target="tpu_custom_call" | custom-call | flops 314572800 | bytes 10485760 | tf_op jit(solution)/shard_map/pallas_call | solution.py:219
  125.3 13.4 %shard_map.114 = (f32[2560,512]{1,0:T(8,128)}, f32[40,512]{1,0:T(8,128)}) custom-call(f32[64,1]{1,0:T(8,128)} %copy.15.rate_ref, f32[8,512]{1,0:T(8,128)} %tf_ref.1, f32[64,64]{1,0:T(8,128)} %coef_ref.1, f32[64,64]{1,0:T(8,128)} %share_ref.1, f32[2560,512]{1,0:T(8,128)} %bitcast.4), custom_call_target="tpu_custom_call" | custom-call | flops 1207959552 | bytes 10485760 | tf_op jit(solution)/shard_map/pallas_call | solution.py:278

commit v3 on v2

--- a/solution.py
+++ b/solution.py
@@ -133,7 +133,7 @@
             ny = jnp.minimum(uy, 0.0)
             for m in range(moments):
                 q = jnp.concatenate([local[s, m], halo[s, m]], axis=0)
-                iv = iv_ref[s * moments + m]
+                iv = iv_ref[m, s]
                 for step in range(SUB):
                     col = lax.broadcasted_iota(jnp.int32, q.shape, 1)
                     western = pltpu.roll(q, 1, 0)
@@ -242,31 +242,44 @@
         cost_estimate=pl.CostEstimate(
             flops=flops, bytes_accessed=4 * (field.size * 2), transcendentals=0
         ),
-    )(speed_x, speed_y, inflow_value.reshape(-1), field, wall_rows, inflow_rows)
+    )(speed_x, speed_y, inflow_value.T, field, wall_rows, inflow_rows)
 
 
 def post_kernel(rate_ref, tf_ref, coef_ref, share_ref, x_ref, spray_ref, gas_ref):
-    span, _ = gas_ref.shape
+    span, strip = gas_ref.shape
     rows = tf_ref.shape[0]
     moments = span // rows
-    sections = rate_ref.shape[0]
-    highest = lax.Precision.HIGHEST
-    rate = rate_ref[...]
-    coef = coef_ref[...]
-    share = share_ref[...]
+    sections = coef_ref.shape[0]
+    highest = lax.Precision.HIGH
+    lane_rows = lax.broadcasted_iota(jnp.int32, (sections, strip), 0)
+    rate = jnp.zeros((sections, strip), jnp.float32)
+    for s in range(sections):
+        rate = jnp.where(lane_rows == s, rate_ref[s], rate)
+    remaining = []
     for r in range(rows):
         factor = rate * tf_ref[pl.ds(r, 1), :]
-        remaining = []
         for m in range(moments):
             x = x_ref[pl.ds(m * rows + r, sections, stride=span), :]
             evaporated = factor * x
             gas_ref[pl.ds(m * rows + r, 1), :] = jnp.sum(evaporated, axis=0, keepdims=True)
             remaining.append(x - evaporated)
-        merge_rate = jnp.dot(coef, remaining[0], precision=highest, preferred_element_type=jnp.float32)
+    mass = jnp.concatenate([remaining[r * moments] for r in range(rows)], axis=1)
+    merge_rate = jnp.dot(coef_ref[...], mass, precision=highest, preferred_element_type=jnp.float32)
+    flux = jnp.concatenate(
+        [
+            remaining[r * moments + m] * merge_rate[:, r * strip : (r + 1) * strip]
+            for r in range(rows)
+            for m in range(moments)
+        ],
+        axis=1,
+    )
+    gained = jnp.dot(share_ref[...], flux, precision=highest, preferred_element_type=jnp.float32)
+    for r in range(rows):
         for m in range(moments):
-            flux = remaining[m] * merge_rate
-            gained = jnp.dot(share, flux, precision=highest, preferred_element_type=jnp.float32)
-            spray_ref[pl.ds(m * rows + r, sections, stride=span), :] = remaining[m] - flux + gained
+            at = (r * moments + m) * strip
+            spray_ref[pl.ds(m * rows + r, sections, stride=span), :] = (
+                remaining[r * moments + m] - flux[:, at : at + strip] + gained[:, at : at + strip]
+            )
 
 
 def evaporate_couple(cell_block, rates, thermal_factor, coefficient, share):
@@ -279,7 +292,7 @@
         post_kernel,
         grid=(block // strip,),
         in_specs=[
-            full((sections, 1)),
+            pl.BlockSpec(memory_space=pltpu.SMEM),
             pl.BlockSpec((rows, strip), lambda i: (0, i)),
             full((sections, sections)),
             full((sections, sections)),
@@ -297,7 +310,7 @@
             flops=2 * sections * sections * flat.size // sections * (moments + 1) // moments * 6,
             bytes_accessed=8 * flat.size, transcendentals=0,
         ),
-    )(rates.reshape(sections, 1), thermal_factor, coefficient, share, flat)
+    )(rates, thermal_factor, coefficient, share, flat)
     return spray.reshape(sections, moments, rows, block), gas.reshape(moments, rows, block)
 
 

time: 139 us -> 131 us (0.942)
  Pallas kernels: 135 us -> 130 us
  local copies, waits for them, and re-layouts: 2.72 us -> 0 us
    pallas_call x1, Pallas kernels: 13.4 us -> 7.93 us  [evaporate_couple(): pl.pallas_call(post_kernel, grid=(block // strip,), in_specs=[pl.BlockSpe...]
    reshape x2 -> x0, local copies, waits for them, and re-layouts: 1.96 us -> none  [the longest x1 1.36 us: evaporate_couple(): rates.reshape(sections, 1)]
where the time goes in v3:
time: 131 us
  Pallas kernels  130 us (99%)
    pallas_call x1, Pallas kernels, transport_exchange(): pl.pallas_call(functools.partial(transport_kernel, groups, lines), out_sh...  122 us
    pallas_call x1, Pallas kernels, evaporate_couple(): pl.pallas_call(post_kernel, grid=(block // strip,), in_specs=[pl.BlockSpe...  7.93 us

profile of v3, /device:TPU:97, one launch (start us, length us, event | category | flops | bytes accessed | tf_op | source)
XLA Modules:
  0.0 130.6 jit_solution(13934741888037137970)
XLA Ops:
  0.6 122.0 %shard_map.113 = f32[64,5,8,512]{3,2,1,0:T(8,128)} custom-call(f32[16]{0:T(128)} %ux_ref.1, f32[16]{0:T(128)} %uy_ref.1, f32[5,16]{1,0:T(8,128)} %bitcast.5, f32[16,5,8,2048]{3,2,1,0:T(8,128)} %field_hbm.1, s32[8,2048]{1,0:T(8,128)} %wall_ref.1, s32[8,2048]{1,0:T(8,128)} %infl_ref.1), custom_call_target="tpu_custom_call" | custom-call | flops 314572800 | bytes 10485760 | tf_op jit(solution)/shard_map/pallas_call | solution.py:219
  122.7 7.9 %shard_map.114 = (f32[2560,512]{1,0:T(8,128)}, f32[40,512]{1,0:T(8,128)}) custom-call(f32[64]{0:T(128)} %rate_ref.1, f32[8,512]{1,0:T(8,128)} %tf_ref.1, f32[64,64]{1,0:T(8,128)} %coef_ref.1, f32[64,64]{1,0:T(8,128)} %share_ref.1, f32[2560,512]{1,0:T(8,128)} %bitcast.4), custom_call_target="tpu_custom_call" | custom-call | flops 1207959552 | bytes 10485760 | tf_op jit(solution)/shard_map/pallas_call | solution.py:291

commit v4 on v3

--- a/solution.py
+++ b/solution.py
@@ -9,6 +9,8 @@
 
 SUB = 4
 CHUNK = 4
+RELAYED = (2, 3)
+PLANE = 4
 MESH = pl.DeviceIdType.MESH
 
 
@@ -16,8 +18,9 @@
     groups, lines,
     ux_ref, uy_ref, iv_ref, field_hbm, wall_ref, infl_ref,
     out_hbm,
-    local, halo, wall_halo, infl_halo, slots,
+    local, halo, wall_halo, infl_halo, slots, relay,
     load_sems, halo_recv, halo_send, mask_recv, mask_send, send_sems, recv_sems, local_sem,
+    relay_recv, relay_send,
 ):
     group_size, moments, rows, columns = field_hbm.shape
     span = 2 * rows
@@ -31,6 +34,21 @@
     east = (me, row + 1)
     first = pl.ds(0, SUB)
     last = pl.ds(SUB, SUB)
+    at = lambda offset: (me, row + offset)
+
+    res = row % PLANE
+    left_edge = (res == PLANE - 1) & (row < lines - 1)
+    right_edge = (res == 0) & (row > 0)
+    east_first = (res == PLANE - 2) & (row + 2 < lines)
+    east_second = (res == PLANE - 2) & (row >= PLANE + 2)
+    west_first = (res == 1) & (row >= PLANE + 1)
+    west_second = (res == 1) & (row + PLANE - 1 < lines)
+    greetings = [
+        (row > 0, -1), (row < lines - 1, 1),
+        (left_edge, -2), (right_edge, 2),
+        (east_first, PLANE), (east_second, -PLANE), (east_second, -2),
+        (west_first, -PLANE), (west_second, PLANE), (west_second, 2),
+    ]
 
     loads = []
     for c in range(chunks):
@@ -54,35 +72,58 @@
     barrier = pltpu.get_barrier_semaphore()
     for d in range(1, groups):
         pl.semaphore_signal(barrier, 1, device_id=(lax.rem(me + d, groups), row), device_id_type=MESH)
-
-    @pl.when(row > 0)
-    def _():
-        pl.semaphore_signal(barrier, 1, device_id=west, device_id_type=MESH)
-
-    @pl.when(row < lines - 1)
-    def _():
-        pl.semaphore_signal(barrier, 1, device_id=east, device_id_type=MESH)
-
-    pl.semaphore_wait(barrier, groups - 1 + has_west + has_east)
-
-    def halo_copy(src, dst, direction, sem_recv, sem_send):
+    for cond, offset in greetings:
+        @pl.when(cond)
+        def _():
+            pl.semaphore_signal(barrier, 1, device_id=at(offset), device_id_type=MESH)
+    same = lambda v: 1 - ((res - v + PLANE) % PLANE + PLANE - 1) // PLANE
+    past = lambda a: (row - a + lines) // lines
+    peers = (
+        groups - 1 + has_west + has_east
+        + same(PLANE - 1) * has_east + same(0) * has_west
+        + same(PLANE - 2) * (1 - past(lines - 2)) + 2 * same(PLANE - 2) * past(PLANE + 2)
+        + same(1) * past(PLANE + 1) + 2 * same(1) * (1 - past(lines - PLANE + 1))
+    )
+    pl.semaphore_wait(barrier, peers)
+
+    def halo_copy(src, dst, target, sem_recv, sem_send):
         return pltpu.make_async_remote_copy(
             src_ref=src, dst_ref=dst, send_sem=sem_send, recv_sem=sem_recv,
-            device_id=west if direction == 0 else east, device_id_type=MESH,
+            device_id=target, device_id_type=MESH,
         )
 
     def field_halo(c, direction):
         part = pl.ds(c * CHUNK, CHUNK)
         if direction == 0:
-            return halo_copy(field_hbm.at[part, :, first, :], halo.at[part, :, first, :], 0,
+            return halo_copy(field_hbm.at[part, :, first, :], halo.at[part, :, first, :], west,
                              halo_recv.at[0, c], halo_send.at[0])
-        return halo_copy(field_hbm.at[part, :, pl.ds(rows - SUB, SUB), :], halo.at[part, :, last, :], 1,
+        return halo_copy(field_hbm.at[part, :, pl.ds(rows - SUB, SUB), :], halo.at[part, :, last, :], east,
                          halo_recv.at[1, c], halo_send.at[1])
+
+    def relay_part(c):
+        return pl.ds(RELAYED.index(c) * CHUNK, CHUNK)
+
+    def relay_in(c, direction):
+        part = pl.ds(c * CHUNK, CHUNK)
+        if direction == 0:
+            return halo_copy(field_hbm.at[part, :, first, :], relay.at[0, relay_part(c)], east,
+                             relay_recv.at[0, RELAYED.index(c)], halo_send.at[0])
+        return halo_copy(field_hbm.at[part, :, pl.ds(rows - SUB, SUB), :], relay.at[0, relay_part(c)], west,
+                         relay_recv.at[0, RELAYED.index(c)], halo_send.at[1])
+
+    def relay_on(c, stage, offset, direction):
+        j = RELAYED.index(c)
+        part = pl.ds(c * CHUNK, CHUNK)
+        if stage == 0:
+            return halo_copy(relay.at[0, relay_part(c)], relay.at[1, relay_part(c)], at(offset),
+                             relay_recv.at[1, j], relay_send.at[0])
+        return halo_copy(relay.at[1, relay_part(c)], halo.at[part, :, first if direction == 0 else last, :],
+                         at(offset), halo_recv.at[direction, c], relay_send.at[1])
 
     def mask_halo(ref, store, k, direction):
         if direction == 0:
-            return halo_copy(ref.at[first, :], store.at[first, :], 0, mask_recv.at[k, 0], mask_send.at[k, 0])
-        return halo_copy(ref.at[pl.ds(rows - SUB, SUB), :], store.at[last, :], 1,
+            return halo_copy(ref.at[first, :], store.at[first, :], west, mask_recv.at[k, 0], mask_send.at[k, 0])
+        return halo_copy(ref.at[pl.ds(rows - SUB, SUB), :], store.at[last, :], east,
                          mask_recv.at[k, 1], mask_send.at[k, 1])
 
     @pl.when(row > 0)
@@ -90,14 +131,32 @@
         mask_halo(wall_ref, wall_halo, 0, 0).start()
         mask_halo(infl_ref, infl_halo, 1, 0).start()
         for c in range(chunks):
-            field_halo(c, 0).start()
+            if c in RELAYED:
+                @pl.when(jnp.logical_not(right_edge))
+                def _():
+                    field_halo(c, 0).start()
+
+                @pl.when(right_edge)
+                def _():
+                    relay_in(c, 0).start()
+            else:
+                field_halo(c, 0).start()
 
     @pl.when(row < lines - 1)
     def _():
         mask_halo(wall_ref, wall_halo, 0, 1).start()
         mask_halo(infl_ref, infl_halo, 1, 1).start()
         for c in range(chunks):
-            field_halo(c, 1).start()
+            if c in RELAYED:
+                @pl.when(jnp.logical_not(left_edge))
+                def _():
+                    field_halo(c, 1).start()
+
+                @pl.when(left_edge)
+                def _():
+                    relay_in(c, 1).start()
+            else:
+                field_halo(c, 1).start()
 
     @pl.when(row < lines - 1)
     def _():
@@ -109,10 +168,37 @@
         mask_halo(wall_ref, wall_halo, 0, 1).wait_recv()
         mask_halo(infl_ref, infl_halo, 1, 1).wait_recv()
 
+    def forward(stage):
+        for c in RELAYED:
+            if stage == 0:
+                @pl.when(east_first)
+                def _():
+                    relay_in(c, 1).wait_recv()
+                    relay_on(c, 0, PLANE, 1).start()
+
+                @pl.when(west_first)
+                def _():
+                    relay_in(c, 0).wait_recv()
+                    relay_on(c, 0, -PLANE, 0).start()
+            else:
+                @pl.when(east_second)
+                def _():
+                    relay_on(c, 0, PLANE, 1).wait_recv()
+                    relay_on(c, 1, -2, 1).start()
+
+                @pl.when(west_second)
+                def _():
+                    relay_on(c, 0, -PLANE, 0).wait_recv()
+                    relay_on(c, 1, 2, 0).start()
+
     def cols_of(k):
         return pl.ds(pl.multiple_of(k * block, block), block)
 
     for c in range(chunks):
+        if c == 1:
+            forward(0)
+        if c == 2:
+            forward(1)
         loads[c].wait()
 
         @pl.when(row < lines - 1)
@@ -172,15 +258,22 @@
     def _():
         mask_halo(wall_ref, wall_halo, 0, 0).wait_send()
         mask_halo(infl_ref, infl_halo, 1, 0).wait_send()
-        halo_copy(field_hbm.at[:, :, first, :], halo.at[:, :, first, :], 0,
+        halo_copy(field_hbm.at[:, :, first, :], halo.at[:, :, first, :], west,
                   halo_recv.at[0, 0], halo_send.at[0]).wait_send()
 
     @pl.when(row < lines - 1)
     def _():
         mask_halo(wall_ref, wall_halo, 0, 1).wait_send()
         mask_halo(infl_ref, infl_halo, 1, 1).wait_send()
-        halo_copy(field_hbm.at[:, :, pl.ds(rows - SUB, SUB), :], halo.at[:, :, last, :], 1,
+        halo_copy(field_hbm.at[:, :, pl.ds(rows - SUB, SUB), :], halo.at[:, :, last, :], east,
                   halo_recv.at[1, 0], halo_send.at[1]).wait_send()
+
+    for stage, conds in ((0, (east_first, west_first)), (1, (east_second, west_second))):
+        for cond in conds:
+            @pl.when(cond)
+            def _():
+                halo_copy(relay.at[stage], relay.at[stage], west,
+                          relay_recv.at[0, 0], relay_send.at[stage]).wait_send()
 
     pltpu.make_async_copy(
         slots.at[:, :, :, cols_of(me)], out_hbm.at[pl.ds(me * group_size, group_size)], local_sem
@@ -227,6 +320,7 @@
             pltpu.VMEM((rows, columns), jnp.int32),
             pltpu.VMEM((rows, columns), jnp.int32),
             pltpu.VMEM((group_size, moments, rows, columns), jnp.float32),
+            pltpu.VMEM((2, len(RELAYED) * CHUNK, moments, SUB, columns), jnp.float32),
             pltpu.SemaphoreType.DMA((chunks,)),
             pltpu.SemaphoreType.DMA((2, chunks)),
             pltpu.SemaphoreType.DMA((2,)),
@@ -235,6 +329,8 @@
             pltpu.SemaphoreType.DMA((groups - 1,)),
             pltpu.SemaphoreType.DMA((groups - 1,)),
             pltpu.SemaphoreType.DMA(()),
+            pltpu.SemaphoreType.DMA((2, len(RELAYED))),
+            pltpu.SemaphoreType.DMA((2,)),
         ],
         compiler_params=pltpu.CompilerParams(
             collective_id=0, has_side_effects=True, vmem_limit_bytes=60 * 1024 * 1024

time: 131 us -> 165 us (1.26)
  Pallas kernels: 130 us -> 163 us
    pallas_call x1, Pallas kernels: 122 us -> 155 us  [transport_exchange(): pl.pallas_call(functools.partial(transport_kernel, groups, lines), out_sh...]
where the time goes in v4:
time: 165 us; the launch traced here: 163 us
  Pallas kernels  163 us (99%)
    pallas_call x1, Pallas kernels, transport_exchange(): pl.pallas_call(functools.partial(transport_kernel, groups, lines), out_sh...  155 us
    pallas_call x1, Pallas kernels, evaporate_couple(): pl.pallas_call(post_kernel, grid=(block // strip,), in_specs=[pl.BlockSpe...  7.92 us

profile of v4, /device:TPU:97, one launch (start us, length us, event | category | flops | bytes accessed | tf_op | source)
XLA Modules:
  0.0 163.3 jit_solution(14267866395832590146)
XLA Ops:
  0.6 154.7 %shard_map.113 = f32[64,5,8,512]{3,2,1,0:T(8,128)} custom-call(f32[16]{0:T(128)} %ux_ref.1, f32[16]{0:T(128)} %uy_ref.1, f32[5,16]{1,0:T(8,128)} %bitcast.5, f32[16,5,8,2048]{3,2,1,0:T(8,128)} %field_hbm.1, s32[8,2048]{1,0:T(8,128)} %wall_ref.1, s32[8,2048]{1,0:T(8,128)} %infl_ref.1), custom_call_target="tpu_custom_call" | custom-call | flops 314572800 | bytes 10485760 | tf_op jit(solution)/shard_map/pallas_call | solution.py:312
  155.4 7.9 %shard_map.114 = (f32[2560,512]{1,0:T(8,128)}, f32[40,512]{1,0:T(8,128)}) custom-call(f32[64]{0:T(128)} %rate_ref.1, f32[8,512]{1,0:T(8,128)} %tf_ref.1, f32[64,64]{1,0:T(8,128)} %coef_ref.1, f32[64,64]{1,0:T(8,128)} %share_ref.1, f32[2560,512]{1,0:T(8,128)} %bitcast.4), custom_call_target="tpu_custom_call" | custom-call | flops 1207959552 | bytes 10485760 | tf_op jit(solution)/shard_map/pallas_call | solution.py:387

commit v5 on v3

--- a/solution.py
+++ b/solution.py
@@ -9,6 +9,8 @@
 
 SUB = 4
 CHUNK = 4
+RELAYED = (2, 3)
+PLANE = 4
 MESH = pl.DeviceIdType.MESH
 
 
@@ -16,8 +18,9 @@
     groups, lines,
     ux_ref, uy_ref, iv_ref, field_hbm, wall_ref, infl_ref,
     out_hbm,
-    local, halo, wall_halo, infl_halo, slots,
+    local, halo, wall_halo, infl_halo, slots, relay,
     load_sems, halo_recv, halo_send, mask_recv, mask_send, send_sems, recv_sems, local_sem,
+    relay_recv, relay_send,
 ):
     group_size, moments, rows, columns = field_hbm.shape
     span = 2 * rows
@@ -31,6 +34,11 @@
     east = (me, row + 1)
     first = pl.ds(0, SUB)
     last = pl.ds(SUB, SUB)
+    res = row % PLANE
+    edge_low = (res == PLANE - 1) & (row < lines - 1)
+    edge_high = (res == 0) & (row > 0)
+    relay_low = (res == PLANE - 2) & (row + 2 < lines)
+    relay_high = (res == 1) & (row >= PLANE + 1)
 
     loads = []
     for c in range(chunks):
@@ -152,21 +160,92 @@
         lax.fori_loop(0, CHUNK, body, 0)
 
         part = pl.ds(c * CHUNK, CHUNK)
-        for d in range(1, groups):
-            k = lax.rem(me + d, groups)
-            pltpu.make_async_remote_copy(
-                src_ref=slots.at[part, :, :, cols_of(k)],
-                dst_ref=out_hbm.at[pl.ds(me * group_size + c * CHUNK, CHUNK)],
-                send_sem=send_sems.at[d - 1],
-                recv_sem=recv_sems.at[d - 1],
-                device_id=(k, row),
-                device_id_type=MESH,
-            ).start()
+
+        def direct():
+            for d in range(1, groups):
+                k = lax.rem(me + d, groups)
+                pltpu.make_async_remote_copy(
+                    src_ref=slots.at[part, :, :, cols_of(k)],
+                    dst_ref=out_hbm.at[pl.ds(me * group_size + c * CHUNK, CHUNK)],
+                    send_sem=send_sems.at[d - 1],
+                    recv_sem=recv_sems.at[d - 1],
+                    device_id=(k, row),
+                    device_id_type=MESH,
+                ).start()
+
+        if c in RELAYED:
+            j = RELAYED.index(c)
+
+            def via(offset):
+                for d in range(1, groups):
+                    k = lax.rem(me + d, groups)
+                    pltpu.make_async_remote_copy(
+                        src_ref=slots.at[part, :, :, cols_of(k)],
+                        dst_ref=relay.at[0, j, d - 1],
+                        send_sem=send_sems.at[d - 1],
+                        recv_sem=relay_recv.at[0, j, d - 1],
+                        device_id=(me, row + offset),
+                        device_id_type=MESH,
+                    ).start()
+
+            pl.when(edge_low)(lambda: via(-1))
+            pl.when(edge_high)(lambda: via(1))
+            pl.when(jnp.logical_not(edge_low | edge_high))(direct)
+        else:
+            direct()
         pltpu.make_async_copy(
             slots.at[part, :, :, cols_of(me)],
             out_hbm.at[pl.ds(me * group_size + c * CHUNK, CHUNK)],
             local_sem,
         ).start()
+
+    def forward(offset):
+        for j in range(len(RELAYED)):
+            for d in range(1, groups):
+                pltpu.make_async_remote_copy(
+                    src_ref=slots.at[pl.ds(0, CHUNK), :, :, cols_of(me)],
+                    dst_ref=relay.at[0, j, d - 1],
+                    send_sem=relay_send.at[0],
+                    recv_sem=relay_recv.at[0, j, d - 1],
+                    device_id=(me, row + offset),
+                    device_id_type=MESH,
+                ).wait_recv()
+                pltpu.make_async_remote_copy(
+                    src_ref=relay.at[0, j, d - 1],
+                    dst_ref=relay.at[1, j, d - 1],
+                    send_sem=relay_send.at[0],
+                    recv_sem=relay_recv.at[1, j, d - 1],
+                    device_id=(lax.rem(me + d, groups), row),
+                    device_id_type=MESH,
+                ).start()
+        for j, c in enumerate(RELAYED):
+            for d in range(1, groups):
+                source = lax.rem(me + groups - d, groups)
+                pltpu.make_async_remote_copy(
+                    src_ref=relay.at[0, j, d - 1],
+                    dst_ref=relay.at[1, j, d - 1],
+                    send_sem=relay_send.at[0],
+                    recv_sem=relay_recv.at[1, j, d - 1],
+                    device_id=(me, row),
+                    device_id_type=MESH,
+                ).wait_recv()
+                pltpu.make_async_remote_copy(
+                    src_ref=relay.at[1, j, d - 1],
+                    dst_ref=out_hbm.at[pl.ds(source * group_size + c * CHUNK, CHUNK)],
+                    send_sem=relay_send.at[1],
+                    recv_sem=recv_sems.at[d - 1],
+                    device_id=(me, row + offset),
+                    device_id_type=MESH,
+                ).start()
+        for stage in range(2):
+            pltpu.make_async_remote_copy(
+                src_ref=relay.at[stage], dst_ref=relay.at[stage],
+                send_sem=relay_send.at[stage], recv_sem=relay_recv.at[stage, 0, 0],
+                device_id=(me, row + offset), device_id_type=MESH,
+            ).wait_send()
+
+    pl.when(relay_low)(lambda: forward(1))
+    pl.when(relay_high)(lambda: forward(-1))
 
     @pl.when(row > 0)
     def _():
@@ -227,6 +306,7 @@
             pltpu.VMEM((rows, columns), jnp.int32),
             pltpu.VMEM((rows, columns), jnp.int32),
             pltpu.VMEM((group_size, moments, rows, columns), jnp.float32),
+            pltpu.VMEM((2, len(RELAYED), groups - 1, CHUNK, moments, rows, block), jnp.float32),
             pltpu.SemaphoreType.DMA((chunks,)),
             pltpu.SemaphoreType.DMA((2, chunks)),
             pltpu.SemaphoreType.DMA((2,)),
@@ -235,6 +315,8 @@
             pltpu.SemaphoreType.DMA((groups - 1,)),
             pltpu.SemaphoreType.DMA((groups - 1,)),
             pltpu.SemaphoreType.DMA(()),
+            pltpu.SemaphoreType.DMA((2, len(RELAYED), groups - 1)),
+            pltpu.SemaphoreType.DMA((2,)),
         ],
         compiler_params=pltpu.CompilerParams(
             collective_id=0, has_side_effects=True, vmem_limit_bytes=60 * 1024 * 1024

time: 131 us -> 159 us (1.21); the launches traced: 131 us -> 156 us
  Pallas kernels: 130 us -> 156 us
    pallas_call x1, Pallas kernels: 122 us -> 148 us  [transport_exchange(): pl.pallas_call(functools.partial(transport_kernel, groups, lines), out_sh...]
where the time goes in v5:
time: 159 us; the launch traced here: 156 us
  Pallas kernels  156 us (98%)
    pallas_call x1, Pallas kernels, transport_exchange(): pl.pallas_call(functools.partial(transport_kernel, groups, lines), out_sh...  148 us
    pallas_call x1, Pallas kernels, evaporate_couple(): pl.pallas_call(post_kernel, grid=(block // strip,), in_specs=[pl.BlockSpe...  7.93 us

profile of v5, /device:TPU:97, one launch (start us, length us, event | category | flops | bytes accessed | tf_op | source)
XLA Modules:
  0.0 156.4 jit_solution(2639635294274378992)
XLA Ops:
  0.6 147.9 %shard_map.113 = f32[64,5,8,512]{3,2,1,0:T(8,128)} custom-call(f32[16]{0:T(128)} %ux_ref.1, f32[16]{0:T(128)} %uy_ref.1, f32[5,16]{1,0:T(8,128)} %bitcast.5, f32[16,5,8,2048]{3,2,1,0:T(8,128)} %field_hbm.1, s32[8,2048]{1,0:T(8,128)} %wall_ref.1, s32[8,2048]{1,0:T(8,128)} %infl_ref.1), custom_call_target="tpu_custom_call" | custom-call | flops 314572800 | bytes 10485760 | tf_op jit(solution)/shard_map/pallas_call | solution.py:298
  148.5 7.9 %shard_map.114 = (f32[2560,512]{1,0:T(8,128)}, f32[40,512]{1,0:T(8,128)}) custom-call(f32[64]{0:T(128)} %rate_ref.1, f32[8,512]{1,0:T(8,128)} %tf_ref.1, f32[64,64]{1,0:T(8,128)} %coef_ref.1, f32[64,64]{1,0:T(8,128)} %share_ref.1, f32[2560,512]{1,0:T(8,128)} %bitcast.4), custom_call_target="tpu_custom_call" | custom-call | flops 1207959552 | bytes 10485760 | tf_op jit(solution)/shard_map/pallas_call | solution.py:373

commit v6 on v3

--- a/solution.py
+++ b/solution.py
@@ -8,7 +8,7 @@
 from jax.sharding import PartitionSpec as P
 
 SUB = 4
-CHUNK = 4
+CHUNK = 2
 MESH = pl.DeviceIdType.MESH
 
 

time: 131 us -> 131 us (level)
  no operation moved by 1% of the time
where the time goes in v6:
time: 131 us
  Pallas kernels  130 us (99%)
    pallas_call x1, Pallas kernels, transport_exchange(): pl.pallas_call(functools.partial(transport_kernel, groups, lines), out_sh...  122 us
    pallas_call x1, Pallas kernels, evaporate_couple(): pl.pallas_call(post_kernel, grid=(block // strip,), in_specs=[pl.BlockSpe...  7.92 us

profile of v6, /device:TPU:97, one launch (start us, length us, event | category | flops | bytes accessed | tf_op | source)
XLA Modules:
  0.0 130.7 jit_solution(9448302551318677303)
XLA Ops:
  0.6 122.2 %shard_map.113 = f32[64,5,8,512]{3,2,1,0:T(8,128)} custom-call(f32[16]{0:T(128)} %ux_ref.1, f32[16]{0:T(128)} %uy_ref.1, f32[5,16]{1,0:T(8,128)} %bitcast.5, f32[16,5,8,2048]{3,2,1,0:T(8,128)} %field_hbm.1, s32[8,2048]{1,0:T(8,128)} %wall_ref.1, s32[8,2048]{1,0:T(8,128)} %infl_ref.1), custom_call_target="tpu_custom_call" | custom-call | flops 314572800 | bytes 10485760 | tf_op jit(solution)/shard_map/pallas_call | solution.py:219
  122.8 7.9 %shard_map.114 = (f32[2560,512]{1,0:T(8,128)}, f32[40,512]{1,0:T(8,128)}) custom-call(f32[64]{0:T(128)} %rate_ref.1, f32[8,512]{1,0:T(8,128)} %tf_ref.1, f32[64,64]{1,0:T(8,128)} %coef_ref.1, f32[64,64]{1,0:T(8,128)} %share_ref.1, f32[2560,512]{1,0:T(8,128)} %bitcast.4), custom_call_target="tpu_custom_call" | custom-call | flops 1207959552 | bytes 10485760 | tf_op jit(solution)/shard_map/pallas_call | solution.py:291

commit v7 on v6

--- a/solution.py
+++ b/solution.py
@@ -9,6 +9,7 @@
 
 SUB = 4
 CHUNK = 2
+AHEAD = 2
 MESH = pl.DeviceIdType.MESH
 
 
@@ -85,19 +86,27 @@
         return halo_copy(ref.at[pl.ds(rows - SUB, SUB), :], store.at[last, :], 1,
                          mask_recv.at[k, 1], mask_send.at[k, 1])
 
+    def send_halos(c):
+        @pl.when(row > 0)
+        def _():
+            field_halo(c, 0).start()
+
+        @pl.when(row < lines - 1)
+        def _():
+            field_halo(c, 1).start()
+
     @pl.when(row > 0)
     def _():
         mask_halo(wall_ref, wall_halo, 0, 0).start()
         mask_halo(infl_ref, infl_halo, 1, 0).start()
-        for c in range(chunks):
-            field_halo(c, 0).start()
 
     @pl.when(row < lines - 1)
     def _():
         mask_halo(wall_ref, wall_halo, 0, 1).start()
         mask_halo(infl_ref, infl_halo, 1, 1).start()
-        for c in range(chunks):
-            field_halo(c, 1).start()
+
+    for c in range(min(AHEAD, chunks)):
+        send_halos(c)
 
     @pl.when(row < lines - 1)
     def _():
@@ -113,6 +122,8 @@
         return pl.ds(pl.multiple_of(k * block, block), block)
 
     for c in range(chunks):
+        if c + AHEAD < chunks:
+            send_halos(c + AHEAD)
         loads[c].wait()
 
         @pl.when(row < lines - 1)

time: 131 us -> 131 us (level)
  no operation moved by 1% of the time
where the time goes in v7:
time: 131 us
  Pallas kernels  130 us (99%)
    pallas_call x1, Pallas kernels, transport_exchange(): pl.pallas_call(functools.partial(transport_kernel, groups, lines), out_sh...  122 us
    pallas_call x1, Pallas kernels, evaporate_couple(): pl.pallas_call(post_kernel, grid=(block // strip,), in_specs=[pl.BlockSpe...  7.93 us

profile of v7, /device:TPU:97, one launch (start us, length us, event | category | flops | bytes accessed | tf_op | source)
XLA Modules:
  0.0 130.7 jit_solution(17122005627352175850)
XLA Ops:
  0.6 122.2 %shard_map.113 = f32[64,5,8,512]{3,2,1,0:T(8,128)} custom-call(f32[16]{0:T(128)} %ux_ref.1, f32[16]{0:T(128)} %uy_ref.1, f32[5,16]{1,0:T(8,128)} %bitcast.5, f32[16,5,8,2048]{3,2,1,0:T(8,128)} %field_hbm.1, s32[8,2048]{1,0:T(8,128)} %wall_ref.1, s32[8,2048]{1,0:T(8,128)} %infl_ref.1), custom_call_target="tpu_custom_call" | custom-call | flops 314572800 | bytes 10485760 | tf_op jit(solution)/shard_map/pallas_call | solution.py:230
  122.8 7.9 %shard_map.114 = (f32[2560,512]{1,0:T(8,128)}, f32[40,512]{1,0:T(8,128)}) custom-call(f32[64]{0:T(128)} %rate_ref.1, f32[8,512]{1,0:T(8,128)} %tf_ref.1, f32[64,64]{1,0:T(8,128)} %coef_ref.1, f32[64,64]{1,0:T(8,128)} %share_ref.1, f32[2560,512]{1,0:T(8,128)} %bitcast.4), custom_call_target="tpu_custom_call" | custom-call | flops 1207959552 | bytes 10485760 | tf_op jit(solution)/shard_map/pallas_call | solution.py:302

commit v8 on v5

--- a/solution.py
+++ b/solution.py
@@ -71,7 +71,19 @@
     def _():
         pl.semaphore_signal(barrier, 1, device_id=east, device_id_type=MESH)
 
-    pl.semaphore_wait(barrier, groups - 1 + has_west + has_east)
+    for d in range(1, groups):
+        partner = lax.rem(me + d, groups)
+        for cond, offset in ((relay_low, 1), (relay_high, -1), (edge_low, -1), (edge_high, 1)):
+            @pl.when(cond)
+            def _():
+                pl.semaphore_signal(barrier, 1, device_id=(partner, row + offset), device_id_type=MESH)
+    same = lambda v: 1 - ((res - v + PLANE) % PLANE + PLANE - 1) // PLANE
+    past = lambda a: (row - a + lines) // lines
+    crossing = (
+        same(PLANE - 1) * has_east + same(0) * has_west
+        + same(PLANE - 2) * (1 - past(lines - 2)) + same(1) * past(PLANE + 1)
+    )
+    pl.semaphore_wait(barrier, groups - 1 + has_west + has_east + (groups - 1) * crossing)
 
     def halo_copy(src, dst, direction, sem_recv, sem_send):
         return pltpu.make_async_remote_copy(
@@ -120,7 +132,32 @@
     def cols_of(k):
         return pl.ds(pl.multiple_of(k * block, block), block)
 
+    def forward(offset, j):
+        c = RELAYED[j]
+        for d in range(1, groups):
+            pltpu.make_async_remote_copy(
+                src_ref=slots.at[pl.ds(0, CHUNK), :, :, cols_of(me)],
+                dst_ref=relay.at[0, j, d - 1],
+                send_sem=relay_send.at[0],
+                recv_sem=relay_recv.at[0, j, d - 1],
+                device_id=(me, row + offset),
+                device_id_type=MESH,
+            ).wait_recv()
+            pltpu.make_async_remote_copy(
+                src_ref=relay.at[0, j, d - 1],
+                dst_ref=out_hbm.at[pl.ds(me * group_size + c * CHUNK, CHUNK)],
+                send_sem=relay_send.at[0],
+                recv_sem=recv_sems.at[d - 1],
+                device_id=(lax.rem(me + d, groups), row + offset),
+                device_id_type=MESH,
+            ).start()
+
+
     for c in range(chunks):
+        if c == chunks - 1:
+            for j in range(len(RELAYED) - 1):
+                pl.when(relay_low)(functools.partial(forward, 1, j))
+                pl.when(relay_high)(functools.partial(forward, -1, j))
         loads[c].wait()
 
         @pl.when(row < lines - 1)
@@ -199,53 +236,19 @@
             local_sem,
         ).start()
 
-    def forward(offset):
-        for j in range(len(RELAYED)):
-            for d in range(1, groups):
-                pltpu.make_async_remote_copy(
-                    src_ref=slots.at[pl.ds(0, CHUNK), :, :, cols_of(me)],
-                    dst_ref=relay.at[0, j, d - 1],
-                    send_sem=relay_send.at[0],
-                    recv_sem=relay_recv.at[0, j, d - 1],
-                    device_id=(me, row + offset),
-                    device_id_type=MESH,
-                ).wait_recv()
-                pltpu.make_async_remote_copy(
-                    src_ref=relay.at[0, j, d - 1],
-                    dst_ref=relay.at[1, j, d - 1],
-                    send_sem=relay_send.at[0],
-                    recv_sem=relay_recv.at[1, j, d - 1],
-                    device_id=(lax.rem(me + d, groups), row),
-                    device_id_type=MESH,
-                ).start()
-        for j, c in enumerate(RELAYED):
-            for d in range(1, groups):
-                source = lax.rem(me + groups - d, groups)
-                pltpu.make_async_remote_copy(
-                    src_ref=relay.at[0, j, d - 1],
-                    dst_ref=relay.at[1, j, d - 1],
-                    send_sem=relay_send.at[0],
-                    recv_sem=relay_recv.at[1, j, d - 1],
-                    device_id=(me, row),
-                    device_id_type=MESH,
-                ).wait_recv()
-                pltpu.make_async_remote_copy(
-                    src_ref=relay.at[1, j, d - 1],
-                    dst_ref=out_hbm.at[pl.ds(source * group_size + c * CHUNK, CHUNK)],
-                    send_sem=relay_send.at[1],
-                    recv_sem=recv_sems.at[d - 1],
-                    device_id=(me, row + offset),
-                    device_id_type=MESH,
-                ).start()
-        for stage in range(2):
-            pltpu.make_async_remote_copy(
-                src_ref=relay.at[stage], dst_ref=relay.at[stage],
-                send_sem=relay_send.at[stage], recv_sem=relay_recv.at[stage, 0, 0],
-                device_id=(me, row + offset), device_id_type=MESH,
-            ).wait_send()
-
-    pl.when(relay_low)(lambda: forward(1))
-    pl.when(relay_high)(lambda: forward(-1))
+    pl.when(relay_low)(lambda: forward(1, len(RELAYED) - 1))
+    pl.when(relay_high)(lambda: forward(-1, len(RELAYED) - 1))
+
+    def settle(offset):
+        pltpu.make_async_remote_copy(
+            src_ref=relay.at[0], dst_ref=relay.at[0],
+            send_sem=relay_send.at[0], recv_sem=relay_recv.at[0, 0, 0],
+            device_id=(me, row + offset), device_id_type=MESH,
+        ).wait_send()
+
+    pl.when(relay_low)(lambda: settle(1))
+    pl.when(relay_high)(lambda: settle(-1))
+
 
     @pl.when(row > 0)
     def _():
@@ -306,7 +309,7 @@
             pltpu.VMEM((rows, columns), jnp.int32),
             pltpu.VMEM((rows, columns), jnp.int32),
             pltpu.VMEM((group_size, moments, rows, columns), jnp.float32),
-            pltpu.VMEM((2, len(RELAYED), groups - 1, CHUNK, moments, rows, block), jnp.float32),
+            pltpu.VMEM((1, len(RELAYED), groups - 1, CHUNK, moments, rows, block), jnp.float32),
             pltpu.SemaphoreType.DMA((chunks,)),
             pltpu.SemaphoreType.DMA((2, chunks)),
             pltpu.SemaphoreType.DMA((2,)),
@@ -315,8 +318,8 @@
             pltpu.SemaphoreType.DMA((groups - 1,)),
             pltpu.SemaphoreType.DMA((groups - 1,)),
             pltpu.SemaphoreType.DMA(()),
-            pltpu.SemaphoreType.DMA((2, len(RELAYED), groups - 1)),
-            pltpu.SemaphoreType.DMA((2,)),
+            pltpu.SemaphoreType.DMA((1, len(RELAYED), groups - 1)),
+            pltpu.SemaphoreType.DMA((1,)),
         ],
         compiler_params=pltpu.CompilerParams(
             collective_id=0, has_side_effects=True, vmem_limit_bytes=60 * 1024 * 1024

time: 159 us -> 135 us (0.85)
  Pallas kernels: 156 us -> 133 us
    pallas_call x1, Pallas kernels: 148 us -> 125 us  [transport_exchange(): pl.pallas_call(functools.partial(transport_kernel, groups, lines), out_sh...]
where the time goes in v8:
time: 135 us; the launch traced here: 134 us
  Pallas kernels  133 us (99%)
    pallas_call x1, Pallas kernels, transport_exchange(): pl.pallas_call(functools.partial(transport_kernel, groups, lines), out_sh...  125 us
    pallas_call x1, Pallas kernels, evaporate_couple(): pl.pallas_call(post_kernel, grid=(block // strip,), in_specs=[pl.BlockSpe...  7.92 us

profile of v8, /device:TPU:97, one launch (start us, length us, event | category | flops | bytes accessed | tf_op | source)
XLA Modules:
  0.0 133.7 jit_solution(16772110176175165012)
XLA Ops:
  0.6 125.2 %shard_map.113 = f32[64,5,8,512]{3,2,1,0:T(8,128)} custom-call(f32[16]{0:T(128)} %ux_ref.1, f32[16]{0:T(128)} %uy_ref.1, f32[5,16]{1,0:T(8,128)} %bitcast.5, f32[16,5,8,2048]{3,2,1,0:T(8,128)} %field_hbm.1, s32[8,2048]{1,0:T(8,128)} %wall_ref.1, s32[8,2048]{1,0:T(8,128)} %infl_ref.1), custom_call_target="tpu_custom_call" | custom-call | flops 314572800 | bytes 10485760 | tf_op jit(solution)/shard_map/pallas_call | solution.py:301
  125.8 7.9 %shard_map.114 = (f32[2560,512]{1,0:T(8,128)}, f32[40,512]{1,0:T(8,128)}) custom-call(f32[64]{0:T(128)} %rate_ref.1, f32[8,512]{1,0:T(8,128)} %tf_ref.1, f32[64,64]{1,0:T(8,128)} %coef_ref.1, f32[64,64]{1,0:T(8,128)} %share_ref.1, f32[2560,512]{1,0:T(8,128)} %bitcast.4), custom_call_target="tpu_custom_call" | custom-call | flops 1207959552 | bytes 10485760 | tf_op jit(solution)/shard_map/pallas_call | solution.py:376
